TPU v7x, 32 devices: a whole 2x2x4 slice. The times are simulated.
32 devices in a mesh: fsdp: 2 (over core), ctx: 4 (over y, x), tp: 4 (over z).
Axes of the slice: x: 2, y: 2, z: 4, core: 2. Of those that a mesh axis runs over, the one named last changes fastest.
Arguments:
- layer_input: float32 [4, 1024, 512], P('fsdp', 'ctx'), may hold values from -6 to 6
- timesteps: int32 [4], P('fsdp'), may hold values from 0 to 999
- segment_ids: int32 [4, 1024], P('fsdp'), may hold values from 0 to 15, never falling along the last dimension, each value on 1 to 512 neighbouring positions
- time_table: float32 [1000, 512], replicated, may hold values from -3 to 3
- ln1_gain: float32 [512], replicated, may hold values from 0.5 to 1.5
- ln1_bias: float32 [512], replicated, may hold values from -1.5 to 1.5
- w_qkv: float32 [3, 512, 512], P(None, 'fsdp', 'tp'), may hold values from -0.25 to 0.25
- b_qv: float32 [2, 512], P(None, 'tp'), may hold values from -1.5 to 1.5
- w_out_t: float32 [512, 512], P('fsdp', 'tp'), may hold values from -1 to 1
- b_out: float32 [512], replicated, may hold values from -1.5 to 1.5
- ln2_gain: float32 [512], replicated, may hold values from 0.5 to 1.5
- ln2_bias: float32 [512], replicated, may hold values from -1.5 to 1.5
- w_up: float32 [512, 2048], P('fsdp', 'tp'), may hold values from -0.25 to 0.25
- b_up: float32 [2048], P('tp'), may hold values from -1.5 to 1.5
- w_down_t: float32 [512, 2048], P('fsdp', 'tp'), may hold values from -0.125 to 0.125
- b_down: float32 [512], replicated, may hold values from -1.5 to 1.5
- out_grad: float32 [4, 1024, 512], P('fsdp', 'ctx'), may hold values from -6 to 6
Outputs:
- output: float32 [4, 1024, 512], P('fsdp', 'ctx')
- grad_input: float32 [4, 1024, 512], P('fsdp', 'ctx')
- grad_table: float32 [1000, 512], replicated
- grad_ln1_gain: float32 [512], replicated
- grad_ln1_bias: float32 [512], replicated
- grad_w_qkv: float32 [3, 512, 512], P(None, 'fsdp', 'tp')
- grad_b_qv: float32 [2, 512], P(None, 'tp')
- grad_w_out_t: float32 [512, 512], P('fsdp', 'tp')
- grad_b_out: float32 [512], replicated
- grad_ln2_gain: float32 [512], replicated
- grad_ln2_bias: float32 [512], replicated
- grad_w_up: float32 [512, 2048], P('fsdp', 'tp')
- grad_b_up: float32 [2048], P('tp')
- grad_w_down_t: float32 [512, 2048], P('fsdp', 'tp')
- grad_b_down: float32 [512], replicated
Inputs may be any that keep to these rules, and one draw needn't show every extreme that they name: `segment_ids`: in each sequence the ids never fall; each document has 1 to 512 characters and one has exactly 512.
All inputs are finite; a program needn't handle non-finite values.
Results may differ from a plain program's by a relative error of at most 0.011.
Values may be sent and summed in bfloat16 or wider, within the bound.
No kernel may reach another device: no remote copies, remote signals or barrier semaphores. Data moves between devices by JAX's collectives and lax.ppermute only.
A program may use at most 64 MiB of HBM per device.

v0:
```python
import jax
import jax.numpy as jnp
from jax import lax
from jax.sharding import PartitionSpec as P

HEAD_DIM = 64
EPSILON = 1e-05
NEGATIVE = -1e30
PRECISE = lax.Precision.HIGHEST


def layer_norm(values, norm_gain, norm_bias):
    centre = values - jnp.mean(values, axis=-1, keepdims=True)
    spread = jnp.mean(centre * centre, axis=-1, keepdims=True)
    return centre * lax.rsqrt(spread + EPSILON) * norm_gain + norm_bias


def contract_last(left, right):
    return lax.dot_general(
        left, right, (((1,), (1,)), ((), ())), preferred_element_type=jnp.float32
    )


def contract_first(left, right):
    return lax.dot_general(
        left, right, (((0,), (0,)), ((), ())), preferred_element_type=jnp.float32
    )


def per_device(
    layer_input,
    timesteps,
    segment_ids,
    time_table,
    ln1_gain,
    ln1_bias,
    w_qkv,
    b_qv,
    w_out_t,
    b_out,
    ln2_gain,
    ln2_bias,
    w_up,
    b_up,
    w_down_t,
    b_down,
    out_grad,
):
    seq_count, span_len, model_width = layer_input.shape
    tok_rows = seq_count * span_len
    seq_len = segment_ids.shape[1]
    step_count = time_table.shape[0]
    ctx_index = lax.axis_index("ctx")
    masters = (
        w_qkv.astype(jnp.bfloat16),
        w_out_t.astype(jnp.bfloat16),
        w_up.astype(jnp.bfloat16),
        w_down_t.astype(jnp.bfloat16),
    )
    qkv_mat, out_mat, up_mat, down_mat = (
        lax.all_gather(masters[0], "fsdp", axis=1, tiled=True),
        lax.all_gather(masters[1], "fsdp", axis=0, tiled=True),
        lax.all_gather(masters[2], "fsdp", axis=0, tiled=True),
        lax.all_gather(masters[3], "fsdp", axis=0, tiled=True),
    )
    steps_hot = (timesteps[:, None] == jnp.arange(step_count, dtype=jnp.int32)[None, :]).astype(
        jnp.float32
    )
    embedded = jnp.dot(steps_hot, time_table, precision=PRECISE)
    stream = (layer_input + embedded[:, None, :]).reshape(tok_rows, model_width)
    normed, norm_one_pull = jax.vjp(layer_norm, stream, ln1_gain, ln1_bias)
    normed_low = normed.astype(jnp.bfloat16)
    projected = jnp.einsum("rd,kdc->krc", normed_low, qkv_mat, preferred_element_type=jnp.float32)
    local_cols = projected.shape[2]
    heads_here = local_cols // HEAD_DIM
    query = (projected[0] + b_qv[0]).astype(jnp.bfloat16)
    key_local = projected[1].astype(jnp.bfloat16).reshape(seq_count, span_len, local_cols)
    value_local = (
        (projected[2] + b_qv[1]).astype(jnp.bfloat16).reshape(seq_count, span_len, local_cols)
    )
    key_all, value_all = (
        lax.all_gather(key_local, "ctx", axis=1, tiled=True),
        lax.all_gather(value_local, "ctx", axis=1, tiled=True),
    )
    query_ids = lax.dynamic_slice_in_dim(segment_ids, ctx_index * span_len, span_len, 1)
    same_doc = (query_ids[:, :, None] == segment_ids[:, None, :])[:, None]
    query_heads = query.reshape(seq_count, span_len, heads_here, HEAD_DIM)
    key_heads = key_all.reshape(seq_count, seq_len, heads_here, HEAD_DIM)
    value_heads = value_all.reshape(seq_count, seq_len, heads_here, HEAD_DIM)
    scale = HEAD_DIM ** (-0.5)

    def score_block():
        raw_scores = jnp.einsum(
            "sqhd,skhd->shqk", query_heads, key_heads, preferred_element_type=jnp.float32
        )
        return jnp.where(same_doc, raw_scores * scale, NEGATIVE)

    scores = score_block()
    row_top = jnp.max(scores, axis=-1, keepdims=True)
    expd = jnp.exp(scores - row_top)
    row_total = jnp.sum(expd, axis=-1, keepdims=True)
    probs = expd / row_total
    log_total = row_top + jnp.log(row_total)
    mixed = jnp.einsum(
        "shqk,skhd->sqhd",
        probs.astype(jnp.bfloat16),
        value_heads,
        preferred_element_type=jnp.float32,
    )
    mixed = mixed.reshape(tok_rows, local_cols).astype(jnp.bfloat16)
    attn_terms = contract_last(mixed, out_mat)
    attn = lax.psum(attn_terms, "tp")
    resid = stream + attn + b_out
    normed_two, norm_two_pull = jax.vjp(layer_norm, resid, ln2_gain, ln2_bias)
    normed_two_low = normed_two.astype(jnp.bfloat16)
    pre_act = jnp.dot(normed_two_low, up_mat, preferred_element_type=jnp.float32) + b_up
    activ, gelu_pull = jax.vjp(jax.nn.gelu, pre_act)
    activ_low = activ.astype(jnp.bfloat16)
    ffn_terms = contract_last(activ_low, down_mat)
    ffn = lax.psum(ffn_terms.astype(jnp.bfloat16), "tp").astype(jnp.float32)
    output = (resid + ffn + b_down).reshape(seq_count, span_len, model_width)
    cotan = out_grad.reshape(tok_rows, model_width)
    cotan_low = cotan.astype(jnp.bfloat16)
    grad_down = contract_first(cotan_low, activ_low)
    grad_act = jnp.dot(cotan_low, down_mat, preferred_element_type=jnp.float32)
    (grad_pre,) = gelu_pull(grad_act)
    grad_pre_low = grad_pre.astype(jnp.bfloat16)
    grad_upmat = contract_first(normed_two_low, grad_pre_low)
    back_two = lax.psum(contract_last(grad_pre_low, up_mat), "tp")
    resid_back, grad_gain_two, grad_bias_two = norm_two_pull(back_two)
    grad_resid = cotan + resid_back
    grad_resid_low = grad_resid.astype(jnp.bfloat16)
    grad_outmat = contract_first(grad_resid_low, mixed)
    grad_mixed = jnp.dot(grad_resid_low, out_mat, preferred_element_type=jnp.float32).astype(
        jnp.bfloat16
    )
    probs_again = jnp.exp(score_block() - log_total)
    mixed_heads = grad_mixed.reshape(seq_count, span_len, heads_here, HEAD_DIM)
    grad_probs = jnp.einsum(
        "sqhd,skhd->shqk", mixed_heads, value_heads, preferred_element_type=jnp.float32
    )
    inner = jnp.sum(probs_again * grad_probs, axis=-1, keepdims=True)
    grad_raw = (probs_again * (grad_probs - inner) * scale).astype(jnp.bfloat16)
    grad_query = jnp.einsum(
        "shqk,skhd->sqhd", grad_raw, key_heads, preferred_element_type=jnp.float32
    ).reshape(tok_rows, local_cols)
    grad_key_all = jnp.einsum(
        "shqk,sqhd->skhd", grad_raw, query_heads, preferred_element_type=jnp.float32
    ).reshape(seq_count, seq_len, local_cols)
    grad_value_all = jnp.einsum(
        "shqk,sqhd->skhd",
        probs_again.astype(jnp.bfloat16),
        mixed_heads,
        preferred_element_type=jnp.float32,
    ).reshape(seq_count, seq_len, local_cols)
    grad_key, grad_value = (
        lax.psum_scatter(grad_key_all, "ctx", scatter_dimension=1, tiled=True),
        lax.psum_scatter(grad_value_all, "ctx", scatter_dimension=1, tiled=True),
    )
    grad_key = grad_key.reshape(tok_rows, local_cols)
    grad_value = grad_value.reshape(tok_rows, local_cols)
    grad_stack = jnp.stack(
        [
            grad_query.astype(jnp.bfloat16),
            grad_key.astype(jnp.bfloat16),
            grad_value.astype(jnp.bfloat16),
        ]
    )
    grad_qkvmat = jnp.einsum(
        "rd,krc->kdc", normed_low, grad_stack, preferred_element_type=jnp.float32
    )
    back_one = lax.psum(
        jnp.einsum("krc,kdc->rd", grad_stack, qkv_mat, preferred_element_type=jnp.float32), "tp"
    )
    stream_back, grad_gain_one, grad_bias_one = norm_one_pull(back_one)
    grad_input = grad_resid + stream_back
    per_sequence = jnp.sum(grad_input.reshape(seq_count, span_len, model_width), axis=1)
    qv_terms = jnp.stack([jnp.sum(grad_query, axis=0), jnp.sum(grad_value, axis=0)])
    small = lax.psum(
        (
            grad_gain_one,
            grad_bias_one,
            grad_gain_two,
            grad_bias_two,
            qv_terms,
            jnp.sum(grad_pre, axis=0),
            jnp.sum(grad_resid, axis=0),
            jnp.sum(cotan, axis=0),
        ),
        ("fsdp", "ctx"),
    )
    (
        gain_one_sum,
        bias_one_sum,
        gain_two_sum,
        bias_two_sum,
        qv_sum,
        up_bias_sum,
        out_bias_sum,
        down_bias_sum,
    ) = small
    table_terms = jnp.dot(steps_hot.T, per_sequence, precision=PRECISE)
    table_sum = lax.psum(table_terms, ("fsdp", "ctx"))
    weight_terms = (grad_qkvmat, grad_outmat, grad_upmat, grad_down)
    summed = lax.psum((weight_terms[0], weight_terms[1], weight_terms[2], weight_terms[3]), "ctx")
    owned = (
        lax.psum_scatter(summed[0], "fsdp", scatter_dimension=1, tiled=True),
        lax.psum_scatter(summed[1], "fsdp", scatter_dimension=0, tiled=True),
        lax.psum_scatter(summed[2], "fsdp", scatter_dimension=0, tiled=True),
        lax.psum_scatter(summed[3], "fsdp", scatter_dimension=0, tiled=True),
    )
    qkv_owned, out_owned, up_owned, down_owned = owned
    return (
        output,
        grad_input.reshape(seq_count, span_len, model_width),
        table_sum,
        gain_one_sum,
        bias_one_sum,
        qkv_owned,
        qv_sum,
        out_owned,
        out_bias_sum,
        gain_two_sum,
        bias_two_sum,
        up_owned,
        up_bias_sum,
        down_owned,
        down_bias_sum,
    )


def solution(mesh):
    placed = (
        P("fsdp", "ctx", None),
        P("fsdp"),
        P("fsdp", None),
        P(),
        P(),
        P(),
        P(None, "fsdp", "tp"),
        P(None, "tp"),
        P("fsdp", "tp"),
        P(),
        P(),
        P(),
        P("fsdp", "tp"),
        P("tp"),
        P("fsdp", "tp"),
        P(),
        P("fsdp", "ctx", None),
    )
    return jax.shard_map(
        per_device,
        mesh=mesh,
        in_specs=placed,
        out_specs=(
            P("fsdp", "ctx", None),
            P("fsdp", "ctx", None),
            P(),
            P(),
            P(),
            P(None, "fsdp", "tp"),
            P(None, "tp"),
            P("fsdp", "tp"),
            P(),
            P(),
            P(),
            P("fsdp", "tp"),
            P("tp"),
            P("fsdp", "tp"),
            P(),
        ),
        check_vma=False,
    )
```

profile of v0, /device:TPU:0, one launch (start us, length us, event | category | flops | bytes accessed | tf_op | source)
XLA Modules:
  0.0 526.8 jit_solution(3402038133135190457)
XLA Ops:
  8.4 2.2 all_gather.18
  17.8 2.0 all_gather.21
  21.0 2.1 reshape.228
  23.0 1.9 copy.60
  25.0 13.5 %all_gather.20 = bf16[2,1024,128]{2,1,0:T(8,128)(2,1)} all-gather(bf16[2,256,128]{2,1,0:T(8,128)(2,1)} %bitcast.102), channel_id=1, replica_groups=mesh['fsdp'=2,'ctx'=4,'tp'=4] {'ctx'}, dimensions={1}, use_global_device_ids=true | all-gather | bytes 655360 | tf_op jit(solution)/shard_map/all_gather | solution.py:82
  38.5 2.0 copy.61
  41.5 9.8 %all_gather.19 = bf16[2,1024,128]{2,1,0:T(8,128)(2,1)} all-gather(bf16[2,256,128]{2,1,0:T(8,128)(2,1)S(1)} %add_convert_fusion.3), channel_id=1, replica_groups=mesh['fsdp'=2,'ctx'=4,'tp'=4] {'ctx'}, dimensions={1}, use_global_device_ids=true | all-gather | bytes 655360 | tf_op jit(solution)/shard_map/all_gather | solution.py:83
  51.3 2.0 copy.58
  53.4 2.5 fusion.67
  62.4 2.3 all_gather.22
  64.7 2.3 all_gather.23
  70.8 41.6 %all-reduce.9.cloned.1.call-done = f32[512,512]{1,0:T(8,128)} async-done(((f32[512,512]{1,0:T(8,128)}), f32[512,512]{1,0:T(8,128)}) %all-reduce.9.cloned.1.call-update) | async-done | bytes 1048592 | tf_op jit(solution)/shard_map/psum | solution.py:112
  114.3 2.7 fusion.55
  119.3 2.7 convolution_convert_fusion
  122.3 48.4 %all-reduce.13.cloned.1.call-done = f32[512,512]{1,0:T(8,128)} async-done(((f32[512,512]{1,0:T(8,128)}), f32[512,512]{1,0:T(8,128)}) %all-reduce.13.cloned.1.call-update) | async-done | bytes 1048592 | tf_op jit(solution)/shard_map/psum | solution.py:129
  170.6 2.0 multiply_reduce_fusion.1
  172.6 38.1 %all-reduce.11.cloned.1.call-done = bf16[512,512]{1,0:T(8,128)(2,1)} async-done(((bf16[512,512]{1,0:T(8,128)(2,1)}), bf16[512,512]{1,0:T(8,128)(2,1)}) %all-reduce.11.cloned.1.call-update) | async-done | bytes 524304 | tf_op jit(solution)/shard_map/psum | solution.py:120
  210.7 3.2 fusion.59
  216.1 1.7 reshape.230
  217.9 1.7 copy.64
  219.6 4.1 fusion.12
  223.7 3.8 fusion.72
  227.6 12.8 %fusion.7 = f32[2,2,64,1024]{3,2,1,0:T(8,128)} fusion(f32[2,2,256,1024]{3,2,1,0:T(8,128)} %fusion.72, f32[2,2,256,1024]{3,2,1,0:T(8,128)} %copy-done.1, f32[2,2,256]{2,1,0:T(2,128)S(1)} %log_add_fusion, f32[2,256,2,64]{1,3,2,0:T(8,128)} %copy.60, f32[2,64]{1,0:T(2,128)S(1)} %add.179), kind=kOutput, calls=%fused_computation.10 | convolution fusion | flops 141690880 | bytes 9703936 | tf_op jit(solution)/shard_map/shqk,sqhd->skhd/dot_general | solution.py:147
  240.5 2.3 fusion.36
  242.8 2.9 convolution_bitcast_fusion
  245.8 3.1 fusion.39
  248.9 12.1 %fusion.65 = (f32[2,64]{1,0:T(2,128)S(1)}, bf16[2,256,2,64]{1,3,2,0:T(8,128)(2,1)}) fusion(bf16[2,1024,2,64]{1,3,2,0:T(8,128)(2,1)} %bitcast.90, f32[2,2,256,1024]{3,2,1,0:T(8,128)} %fusion.72, f32[2,2,256,1024]{3,2,1,0:T(8,128)} %copy-done.1, f32[2,2,256]{2,1,0:T(2,128)S(1)} %log_add_fusion), kind=kOutput, calls=%fused_computation.104 | convolution fusion | flops 141690752 | bytes 9048576 | tf_op jit(solution)/shard_map/shqk,skhd->sqhd/dot_general | solution.py:144
  261.0 1.8 copy.76
  262.8 1.8 reshape.229
  264.6 1.7 fusion.66
  266.3 1.7 copy.68
  268.0 14.4 %reduce-scatter.7.cloned.1.call-done = f32[2,256,128]{1,2,0:T(8,128)} async-done(((f32[2,1024,128]{1,2,0:T(8,128)}), f32[2,256,128]{1,2,0:T(8,128)}) %reduce-scatter.7.cloned.1.call-update) | async-done | bytes 262160 | tf_op jit(solution)/shard_map/reduce_scatter | solution.py:157
  285.6 2.5 convolution_bitcast_fusion.2
  288.2 2.5 convolution_bitcast_fusion.1
  290.8 1.9 reduce-scatter.13.cloned.1.call-done
  292.7 12.1 %reduce-scatter.17.cloned.1.call-done = f32[256,512]{0,1:T(8,128)} async-done(((f32[512,512]{0,1:T(8,128)}), f32[256,512]{0,1:T(8,128)}) %reduce-scatter.17.cloned.1.call-update) | async-done | bytes 524304 | tf_op jit(solution)/shard_map/reduce_scatter | solution.py:210
  304.8 12.0 %reduce-scatter.15.cloned.1.call-done = f32[256,512]{1,0:T(8,128)} async-done(((f32[512,512]{1,0:T(8,128)}), f32[256,512]{1,0:T(8,128)}) %reduce-scatter.15.cloned.1.call-update) | async-done | bytes 524304 | tf_op jit(solution)/shard_map/reduce_scatter | solution.py:209
  316.7 12.3 %reduce-scatter.11.cloned.1.call-done = f32[3,256,128]{1,2,0:T(8,128)} async-done(((f32[3,512,128]{1,2,0:T(8,128)}), f32[3,256,128]{1,2,0:T(8,128)}) %reduce-scatter.11.cloned.1.call-update) | async-done | bytes 393232 | tf_op jit(solution)/shard_map/reduce_scatter | solution.py:207
  329.4 55.5 %all-reduce.15.cloned.1.call-done = f32[512,512]{1,0:T(8,128)} async-done(((f32[512,512]{1,0:T(8,128)}), f32[512,512]{1,0:T(8,128)}) %all-reduce.15.cloned.1.call-update) | async-done | bytes 1048592 | tf_op jit(solution)/shard_map/psum | solution.py:172
  384.9 1.8 multiply_reduce_fusion.2
  386.7 1.8 fusion.58
  388.7 2.4 fusion.43
  391.2 27.6 %all-reduce = (f32[512]{0:T(512)}, f32[512]{0:T(512)}, f32[2,128]{1,0:T(2,128)}, f32[512]{0:T(512)}, f32[512]{0:T(512)}, /*index=5*/f32[512]{0:T(512)}, f32[512]{0:T(512)}, f32[512]{0:T(512)}) all-reduce(f32[512]{0:T(512)S(1)} %get-tuple-element.62, ...), channel_id=1, replica_groups=mesh['fsdp'=2,'ctx'=4,'tp'=4] {'fsdp','ctx'}, use_global_device_ids=true, to_apply=%region_20.21 | all-reduce | flops 3840 | bytes 30720 | tf_op jit(solution)/shard_map/psum | solution.py:179
  418.9 31.2 %all-reduce.19.cloned.1.call-done = (f32[3,256,128]{1,2,0:T(8,128)}, f32[256,128]{1,0:T(8,128)}, f32[256,512]{1,0:T(8,128)}, f32[256,512]{0,1:T(8,128)}) async-done(((f32[3,256,128]{1,2,0:T(8,128)}, f32[256,128]{1,0:T(8,128)}, f32[256,512]{1,0:T(8,128)}, f32[256,512]{0,1:T(8,128)}), (f32[3,256,128]{1,2,0:T(8,128)}, f32[256,128]{1,0:T(8,128)}, f32[256,512]{1,0:T(8,128)}, ...) | async-done | bytes 1572880 | tf_op jit(solution)/shard_map/psum | solution.py:205
  450.1 1.9 copy.71
  452.1 2.0 copy.72
  454.1 61.3 %all-reduce.17.cloned.1.call-done = f32[1000,512]{1,0:T(8,128)} async-done(((f32[1000,512]{1,0:T(8,128)}), f32[1000,512]{1,0:T(8,128)}) %all-reduce.17.cloned.1.call-update) | async-done | bytes 2048016 | tf_op jit(solution)/shard_map/psum | solution.py:203
  515.4 3.1 copy.92
  (135 shorter events, 33.1 us)
Async XLA Ops:
  7.2 3.4 copy-start
  7.2 6.6 %copy-start.20 = (f32[512]{0:T(512)S(1)}, f32[512]{0:T(512)}, u32[]{:S(2)}) copy-start(f32[512]{0:T(512)} %param.21) | copy-start | bytes 6148
  7.2 6.6 %copy-start.22 = (f32[512]{0:T(512)S(1)}, f32[512]{0:T(512)}, u32[]{:S(2)}) copy-start(f32[512]{0:T(512)} %param.22) | copy-start | bytes 6148
  7.2 105.2 %all-reduce.9.cloned.1.call-start = ((), (), s32[]{:S(2)}) async-start(), calls=%async_computation.6 | async-start | bytes 2097152 | tf_op jit(solution)/shard_map/psum | solution.py:112
  12.0 4.7 copy-start.29
  12.0 7.8 %copy-start.21 = (s32[2,1024]{1,0:T(2,128)S(1)}, s32[2,1024]{1,0:T(2,128)}, u32[]{:S(2)}) copy-start(s32[2,1024]{1,0:T(2,128)} %param.19) | copy-start | bytes 24580
  14.0 0.8 copy-start.5
  53.4 3.6 copy-start.8
  55.8 2.2 copy-start.1
  56.9 1.9 copy-start.13
  58.2 0.7 copy-start.15
  60.1 52.3 %copy-start.23 = (f32[512]{0:T(512)S(1)}, f32[512]{0:T(512)}, u32[]{:S(2)}) copy-start(f32[512]{0:T(512)} %param.26) | copy-start | bytes 6148
  60.2 110.5 %all-reduce.13.cloned.1.call-start = ((), (), s32[]{:S(2)}) async-start(), calls=%async_computation.8 | async-start | bytes 2097152 | tf_op jit(solution)/shard_map/psum | solution.py:129
  64.7 49.5 %copy-start.19 = (f32[512]{0:T(512)S(1)}, f32[512]{0:T(512)}, u32[]{:S(2)}) copy-start(f32[512]{0:T(512)} %param.27) | copy-start | bytes 6148
  64.7 49.6 %copy-start.25 = (f32[512]{0:T(512)S(1)}, f32[512]{0:T(512)}, u32[]{:S(2)}) copy-start(f32[512]{0:T(512)} %param.28) | copy-start | bytes 6148
  64.7 49.6 %copy-start.30 = (f32[512]{0:T(512)S(1)}, f32[512]{0:T(512)}, u32[]{:S(2)}) copy-start(f32[512]{0:T(512)} %param.30) | copy-start | bytes 6148
  67.0 1.6 copy-start.11
  68.6 0.8 copy-start.10
  112.4 1.9 copy-start.12
  112.4 1.9 copy-start.16
  113.9 3.0 copy-start.2
  117.0 0.8 copy-start.9
  117.8 92.9 %copy-start.24 = (f32[512]{0:T(512)S(1)}, f32[512]{0:T(512)}, u32[]{:S(2)}) copy-start(f32[512]{0:T(512)} %param.32) | copy-start | bytes 6148
  119.3 91.4 %all-reduce.11.cloned.1.call-start = ((), (), s32[]{:S(2)}) async-start(), calls=%async_computation.7 | async-start | bytes 1048576 | tf_op jit(solution)/shard_map/psum | solution.py:120
  122.0 142.5 %reduce-scatter.9.cloned.1.call-start = ((), (), s32[]{:S(2)}) async-start(), calls=%async_computation.10 | async-start | bytes 1310720 | tf_op jit(solution)/shard_map/reduce_scatter | solution.py:158
  210.7 3.2 copy-start.6
  210.7 4.5 copy-start.14
  214.1 1.1 copy-start.3
  223.7 58.7 %reduce-scatter.7.cloned.1.call-start = ((), (), s32[]{:S(2)}) async-start(), calls=%async_computation.9 | async-start | bytes 1310720 | tf_op jit(solution)/shard_map/reduce_scatter | solution.py:157
  240.4 5.4 %copy-start.26 = (f32[512]{0:T(512)S(1)}, f32[512]{0:T(512)}, u32[]{:S(2)}) copy-start(f32[512]{0:T(512)} %param.28) | copy-start | bytes 6148
  240.4 52.3 %reduce-scatter.13.cloned.1.call-start = ((), (), s32[]{:S(2)}) async-start(), calls=%async_computation.14 | async-start | bytes 393216 | tf_op jit(solution)/shard_map/reduce_scatter | solution.py:208
  242.7 62.0 %reduce-scatter.17.cloned.1.call-start = ((), (), s32[]{:S(2)}) async-start(), calls=%async_computation.16 | async-start | bytes 1572864 | tf_op jit(solution)/shard_map/reduce_scatter | solution.py:210
  245.7 71.0 %reduce-scatter.15.cloned.1.call-start = ((), (), s32[]{:S(2)}) async-start(), calls=%async_computation.15 | async-start | bytes 1572864 | tf_op jit(solution)/shard_map/reduce_scatter | solution.py:209
  248.9 80.2 %reduce-scatter.11.cloned.1.call-start = ((), (), s32[]{:S(2)}) async-start(), calls=%async_computation.13 | async-start | bytes 1179648 | tf_op jit(solution)/shard_map/reduce_scatter | solution.py:207
  288.2 96.7 %all-reduce.15.cloned.1.call-start = ((), (), s32[]{:S(2)}) async-start(), calls=%async_computation.11 | async-start | bytes 2097152 | tf_op jit(solution)/shard_map/psum | solution.py:172
  290.7 159.4 %all-reduce.19.cloned.1.call-start = ((), (), s32[]{:S(2)}) async-start(), calls=%async_computation.17 | async-start | bytes 3145728 | tf_op jit(solution)/shard_map/psum | solution.py:205
  329.1 186.3 %all-reduce.17.cloned.1.call-start = ((), (), s32[]{:S(2)}) async-start(), calls=%async_computation.12 | async-start | bytes 4096000 | tf_op jit(solution)/shard_map/psum | solution.py:203
  384.9 3.6 copy-start.4
  386.6 2.1 copy-start.27
  388.4 2.8 copy-start.28
  388.6 129.9 %copy-start.7 = (f32[512,512]{1,0:T(8,128)}, f32[512,512]{1,0:T(8,128)S(1)}, u32[]{:S(2)}) copy-start(f32[512,512]{1,0:T(8,128)S(1)} %add_add_fusion.2) | copy-start | bytes 3145732
  450.1 68.4 %copy-start.18 = (f32[256,128]{1,0:T(8,128)S(1)}, f32[256,128]{1,0:T(8,128)}, u32[]{:S(2)}) copy-start(f32[256,128]{1,0:T(8,128)} %get-tuple-element.117) | copy-start | bytes 393220
  515.4 3.8 copy-start.17
Sparse Core Ops, SparseCore 0:
  60.3 52.0 all-reduce.8
  119.4 51.1 all-reduce.12
  173.0 37.6 all-reduce.10
  223.8 27.7 reduce-scatter.8
  254.6 27.7 reduce-scatter.6
  285.0 7.6 reduce-scatter.12
  295.0 9.6 reduce-scatter.16
  307.0 9.6 reduce-scatter.14
  319.7 9.3 reduce-scatter.10
  331.9 52.9 all-reduce.14
  388.6 61.4 all-reduce.18
  453.8 61.5 all-reduce.16
where the time goes:
time: 528 us; the launch traced here: 527 us
  waiting for transfers between devices  329 us (62%)
  matrix products  64.3 us (12%)
  blocking collectives  59.8 us (11%)
  local copies, waits for them, and re-layouts  33 us (6%)
  other arithmetic  25.2 us (5%)
  between operations  14.6 us (3%)
    psum x1, waiting for transfers between devices, per_device(): table_sum = lax.psum(table_terms, ('fsdp', 'ctx'))  61.3 us
    psum x1, waiting for transfers between devices, per_device(): lax.psum(jnp.einsum('krc,kdc->rd', grad_stack, qkv_mat, preferred_element...  55.5 us
    psum x1, waiting for transfers between devices, per_device(): back_two = lax.psum(contract_last(grad_pre_low, up_mat), 'tp')  48.4 us
    psum x1, waiting for transfers between devices, per_device(): attn = lax.psum(attn_terms, 'tp')  41.6 us
    psum x1, waiting for transfers between devices, per_device(): ffn = lax.psum(ffn_terms.astype(jnp.bfloat16), 'tp').astype(jnp.float32)  38.1 us
    psum x1, waiting for transfers between devices, per_device(): lax.psum((weight_terms[0], weight_terms[1], weight_terms[2], weight_terms...  31.2 us
    psum x1, blocking collectives, per_device(): lax.psum((grad_gain_one, grad_bias_one, grad_gain_two, grad_bias_two, qv_...  27.6 us
    reduce_scatter x1, waiting for transfers between devices, per_device(): lax.psum_scatter(grad_key_all, 'ctx', scatter_dimension=1, tiled=True)  14.4 us
  transfers between devices with their start and end apart: 12, of which 11 were waited for; matrix products, arithmetic and copies ran while one was open for 14% of the time, Pallas kernels for 0%

commit v1 on v0

--- a/solution.py
+++ b/solution.py
@@ -176,19 +176,18 @@
     grad_input = grad_resid + stream_back
     per_sequence = jnp.sum(grad_input.reshape(seq_count, span_len, model_width), axis=1)
     qv_terms = jnp.stack([jnp.sum(grad_query, axis=0), jnp.sum(grad_value, axis=0)])
-    small = lax.psum(
-        (
-            grad_gain_one,
-            grad_bias_one,
-            grad_gain_two,
-            grad_bias_two,
-            qv_terms,
-            jnp.sum(grad_pre, axis=0),
-            jnp.sum(grad_resid, axis=0),
-            jnp.sum(cotan, axis=0),
-        ),
-        ("fsdp", "ctx"),
-    )
+    small = (
+        grad_gain_one,
+        grad_bias_one,
+        grad_gain_two,
+        grad_bias_two,
+        qv_terms,
+        jnp.sum(grad_pre, axis=0),
+        jnp.sum(grad_resid, axis=0),
+        jnp.sum(cotan, axis=0),
+    )
+    for mesh_axis in ("fsdp", "ctx"):
+        small = lax.psum(small, mesh_axis)
     (
         gain_one_sum,
         bias_one_sum,

time: 528 us -> 528 us (level)
  blocking collectives: 59.8 us -> 52.3 us
  waiting for transfers between devices: 329 us -> 336 us
    psum x1 -> x2, blocking collectives: 27.6 us -> 20.2 us  [per_device(): small = lax.psum(small, mesh_axis)]
    psum x1, waiting for transfers between devices: 31.2 us -> 38.5 us  [per_device(): lax.psum((weight_terms[0], weight_terms[1], weight_terms[2], weight_terms...]
where the time goes in v1:
time: 528 us; the launch traced here: 527 us
  waiting for transfers between devices  336 us (64%)
  matrix products  64.3 us (12%)
  blocking collectives  52.3 us (10%)
  local copies, waits for them, and re-layouts  33 us (6%)
  other arithmetic  25.2 us (5%)
  between operations  14.6 us (3%)
    psum x1, waiting for transfers between devices, per_device(): table_sum = lax.psum(table_terms, ('fsdp', 'ctx'))  61.3 us
    psum x1, waiting for transfers between devices, per_device(): lax.psum(jnp.einsum('krc,kdc->rd', grad_stack, qkv_mat, preferred_element...  55.5 us
    psum x1, waiting for transfers between devices, per_device(): back_two = lax.psum(contract_last(grad_pre_low, up_mat), 'tp')  48.4 us
    psum x1, waiting for transfers between devices, per_device(): attn = lax.psum(attn_terms, 'tp')  41.6 us
    psum x1, waiting for transfers between devices, per_device(): lax.psum((weight_terms[0], weight_terms[1], weight_terms[2], weight_terms...  38.5 us
    psum x1, waiting for transfers between devices, per_device(): ffn = lax.psum(ffn_terms.astype(jnp.bfloat16), 'tp').astype(jnp.float32)  38.1 us
    psum x2, blocking collectives, per_device(): small = lax.psum(small, mesh_axis)  20.2 us
    reduce_scatter x1, waiting for transfers between devices, per_device(): lax.psum_scatter(grad_key_all, 'ctx', scatter_dimension=1, tiled=True)  14.4 us
  transfers between devices with their start and end apart: 12, of which 11 were waited for; matrix products, arithmetic and copies ran while one was open for 14% of the time, Pallas kernels for 0%

profile of v1, /device:TPU:0, one launch (start us, length us, event | category | flops | bytes accessed | tf_op | source)
XLA Modules:
  0.0 526.6 jit_solution(13752148472991624702)
XLA Ops:
  8.4 2.2 all_gather.18
  17.8 2.0 all_gather.21
  21.0 2.1 reshape.228
  23.0 1.9 copy.60
  25.0 13.5 %all_gather.20 = bf16[2,1024,128]{2,1,0:T(8,128)(2,1)} all-gather(bf16[2,256,128]{2,1,0:T(8,128)(2,1)} %bitcast.102), channel_id=1, replica_groups=mesh['fsdp'=2,'ctx'=4,'tp'=4] {'ctx'}, dimensions={1}, use_global_device_ids=true | all-gather | bytes 655360 | tf_op jit(solution)/shard_map/all_gather | solution.py:82
  38.5 2.0 copy.61
  41.5 9.8 %all_gather.19 = bf16[2,1024,128]{2,1,0:T(8,128)(2,1)} all-gather(bf16[2,256,128]{2,1,0:T(8,128)(2,1)S(1)} %add_convert_fusion.3), channel_id=1, replica_groups=mesh['fsdp'=2,'ctx'=4,'tp'=4] {'ctx'}, dimensions={1}, use_global_device_ids=true | all-gather | bytes 655360 | tf_op jit(solution)/shard_map/all_gather | solution.py:83
  51.3 2.0 copy.58
  53.4 2.5 fusion.67
  62.4 2.3 all_gather.22
  64.7 2.3 all_gather.23
  70.8 41.6 %all-reduce.10.cloned.1.call-done = f32[512,512]{1,0:T(8,128)} async-done(((f32[512,512]{1,0:T(8,128)}), f32[512,512]{1,0:T(8,128)}) %all-reduce.10.cloned.1.call-update) | async-done | bytes 1048592 | tf_op jit(solution)/shard_map/psum | solution.py:112
  114.3 2.7 fusion.55
  119.3 2.7 convolution_convert_fusion
  122.3 48.4 %all-reduce.14.cloned.1.call-done = f32[512,512]{1,0:T(8,128)} async-done(((f32[512,512]{1,0:T(8,128)}), f32[512,512]{1,0:T(8,128)}) %all-reduce.14.cloned.1.call-update) | async-done | bytes 1048592 | tf_op jit(solution)/shard_map/psum | solution.py:129
  170.6 2.0 multiply_reduce_fusion.1
  172.6 38.1 %all-reduce.12.cloned.1.call-done = bf16[512,512]{1,0:T(8,128)(2,1)} async-done(((bf16[512,512]{1,0:T(8,128)(2,1)}), bf16[512,512]{1,0:T(8,128)(2,1)}) %all-reduce.12.cloned.1.call-update) | async-done | bytes 524304 | tf_op jit(solution)/shard_map/psum | solution.py:120
  210.7 3.2 fusion.59
  216.1 1.7 reshape.230
  217.9 1.7 copy.64
  219.6 4.1 fusion.12
  223.7 3.8 fusion.72
  227.6 12.8 %fusion.7 = f32[2,2,64,1024]{3,2,1,0:T(8,128)} fusion(f32[2,2,256,1024]{3,2,1,0:T(8,128)} %fusion.72, f32[2,2,256,1024]{3,2,1,0:T(8,128)} %copy-done.1, f32[2,2,256]{2,1,0:T(2,128)S(1)} %log_add_fusion, f32[2,256,2,64]{1,3,2,0:T(8,128)} %copy.60, f32[2,64]{1,0:T(2,128)S(1)} %add.195), kind=kOutput, calls=%fused_computation.10 | convolution fusion | flops 141690880 | bytes 9703936 | tf_op jit(solution)/shard_map/shqk,sqhd->skhd/dot_general | solution.py:147
  240.5 2.3 fusion.36
  242.8 2.9 convolution_bitcast_fusion
  245.8 3.1 fusion.39
  248.9 12.1 %fusion.65 = (f32[2,64]{1,0:T(2,128)S(1)}, bf16[2,256,2,64]{1,3,2,0:T(8,128)(2,1)}) fusion(bf16[2,1024,2,64]{1,3,2,0:T(8,128)(2,1)} %bitcast.90, f32[2,2,256,1024]{3,2,1,0:T(8,128)} %fusion.72, f32[2,2,256,1024]{3,2,1,0:T(8,128)} %copy-done.1, f32[2,2,256]{2,1,0:T(2,128)S(1)} %log_add_fusion), kind=kOutput, calls=%fused_computation.104 | convolution fusion | flops 141690752 | bytes 9048576 | tf_op jit(solution)/shard_map/shqk,skhd->sqhd/dot_general | solution.py:144
  261.0 1.8 copy.76
  262.8 1.8 reshape.229
  264.6 1.7 fusion.66
  268.0 14.4 %reduce-scatter.7.cloned.1.call-done = f32[2,256,128]{1,2,0:T(8,128)} async-done(((f32[2,1024,128]{1,2,0:T(8,128)}), f32[2,256,128]{1,2,0:T(8,128)}) %reduce-scatter.7.cloned.1.call-update) | async-done | bytes 262160 | tf_op jit(solution)/shard_map/reduce_scatter | solution.py:157
  285.6 2.5 convolution_bitcast_fusion.2
  288.2 2.5 convolution_bitcast_fusion.1
  290.8 1.9 reduce-scatter.13.cloned.1.call-done
  292.7 12.1 %reduce-scatter.17.cloned.1.call-done = f32[256,512]{0,1:T(8,128)} async-done(((f32[512,512]{0,1:T(8,128)}), f32[256,512]{0,1:T(8,128)}) %reduce-scatter.17.cloned.1.call-update) | async-done | bytes 524304 | tf_op jit(solution)/shard_map/reduce_scatter | solution.py:209
  304.8 12.0 %reduce-scatter.15.cloned.1.call-done = f32[256,512]{1,0:T(8,128)} async-done(((f32[512,512]{1,0:T(8,128)}), f32[256,512]{1,0:T(8,128)}) %reduce-scatter.15.cloned.1.call-update) | async-done | bytes 524304 | tf_op jit(solution)/shard_map/reduce_scatter | solution.py:208
  316.7 12.3 %reduce-scatter.11.cloned.1.call-done = f32[3,256,128]{1,2,0:T(8,128)} async-done(((f32[3,512,128]{1,2,0:T(8,128)}), f32[3,256,128]{1,2,0:T(8,128)}) %reduce-scatter.11.cloned.1.call-update) | async-done | bytes 393232 | tf_op jit(solution)/shard_map/reduce_scatter | solution.py:206
  329.4 55.5 %all-reduce.16.cloned.1.call-done = f32[512,512]{1,0:T(8,128)} async-done(((f32[512,512]{1,0:T(8,128)}), f32[512,512]{1,0:T(8,128)}) %all-reduce.16.cloned.1.call-update) | async-done | bytes 1048592 | tf_op jit(solution)/shard_map/psum | solution.py:172
  384.9 1.8 multiply_reduce_fusion.2
  386.7 1.8 fusion.58
  388.7 2.4 fusion.43
  391.2 3.4 all-reduce.2
  394.6 16.8 %all-reduce = (f32[512]{0:T(512)}, f32[512]{0:T(512)}, f32[2,128]{1,0:T(2,128)}, f32[512]{0:T(512)}, f32[512]{0:T(512)}, /*index=5*/f32[512]{0:T(512)}, f32[512]{0:T(512)}, f32[512]{0:T(512)}) all-reduce(f32[512]{0:T(512)S(1)} %get-tuple-element.78, f32[512]{0:T(512)S(1)} %get-tuple-element.79, ...), channel_id=1, replica_groups=mesh['fsdp'=2,'ctx'=4,'tp'=4] {'ctx'}, use_global_device_ids=true, to_apply=%region_21.22 | all-reduce | flops 3840 | bytes 30720 | tf_op jit(solution)/shard_map/psum | solution.py:190
  411.4 38.5 %all-reduce.20.cloned.1.call-done = (f32[3,256,128]{1,2,0:T(8,128)}, f32[256,128]{1,0:T(8,128)}, f32[256,512]{1,0:T(8,128)}, f32[256,512]{0,1:T(8,128)}) async-done(((f32[3,256,128]{1,2,0:T(8,128)}, f32[256,128]{1,0:T(8,128)}, f32[256,512]{1,0:T(8,128)}, f32[256,512]{0,1:T(8,128)}), (f32[3,256,128]{1,2,0:T(8,128)}, f32[256,128]{1,0:T(8,128)}, f32[256,512]{1,0:T(8,128)}, ...) | async-done | bytes 1572880 | tf_op jit(solution)/shard_map/psum | solution.py:204
  449.9 1.9 copy.71
  451.9 2.0 copy.72
  453.9 61.3 %all-reduce.18.cloned.1.call-done = f32[1000,512]{1,0:T(8,128)} async-done(((f32[1000,512]{1,0:T(8,128)}), f32[1000,512]{1,0:T(8,128)}) %all-reduce.18.cloned.1.call-update) | async-done | bytes 2048016 | tf_op jit(solution)/shard_map/psum | solution.py:202
  515.2 3.1 copy.92
  (136 shorter events, 34.8 us)
Async XLA Ops:
  7.2 3.4 copy-start
  7.2 6.6 %copy-start.20 = (f32[512]{0:T(512)S(1)}, f32[512]{0:T(512)}, u32[]{:S(2)}) copy-start(f32[512]{0:T(512)} %param.21) | copy-start | bytes 6148
  7.2 6.6 %copy-start.22 = (f32[512]{0:T(512)S(1)}, f32[512]{0:T(512)}, u32[]{:S(2)}) copy-start(f32[512]{0:T(512)} %param.22) | copy-start | bytes 6148
  7.2 105.2 %all-reduce.10.cloned.1.call-start = ((), (), s32[]{:S(2)}) async-start(), calls=%async_computation.6 | async-start | bytes 2097152 | tf_op jit(solution)/shard_map/psum | solution.py:112
  12.0 4.7 copy-start.29
  12.0 7.8 %copy-start.21 = (s32[2,1024]{1,0:T(2,128)S(1)}, s32[2,1024]{1,0:T(2,128)}, u32[]{:S(2)}) copy-start(s32[2,1024]{1,0:T(2,128)} %param.19) | copy-start | bytes 24580
  14.0 0.8 copy-start.5
  53.4 3.6 copy-start.8
  55.8 2.2 copy-start.1
  56.9 1.9 copy-start.13
  58.2 0.7 copy-start.15
  60.1 52.3 %copy-start.23 = (f32[512]{0:T(512)S(1)}, f32[512]{0:T(512)}, u32[]{:S(2)}) copy-start(f32[512]{0:T(512)} %param.26) | copy-start | bytes 6148
  60.2 110.5 %all-reduce.14.cloned.1.call-start = ((), (), s32[]{:S(2)}) async-start(), calls=%async_computation.8 | async-start | bytes 2097152 | tf_op jit(solution)/shard_map/psum | solution.py:129
  64.7 49.5 %copy-start.19 = (f32[512]{0:T(512)S(1)}, f32[512]{0:T(512)}, u32[]{:S(2)}) copy-start(f32[512]{0:T(512)} %param.27) | copy-start | bytes 6148
  64.7 49.6 %copy-start.25 = (f32[512]{0:T(512)S(1)}, f32[512]{0:T(512)}, u32[]{:S(2)}) copy-start(f32[512]{0:T(512)} %param.28) | copy-start | bytes 6148
  64.7 49.6 %copy-start.30 = (f32[512]{0:T(512)S(1)}, f32[512]{0:T(512)}, u32[]{:S(2)}) copy-start(f32[512]{0:T(512)} %param.30) | copy-start | bytes 6148
  67.0 1.6 copy-start.11
  68.6 0.8 copy-start.10
  112.4 1.9 copy-start.12
  112.4 1.9 copy-start.16
  113.9 3.0 copy-start.2
  117.0 0.8 copy-start.9
  117.8 92.9 %copy-start.24 = (f32[512]{0:T(512)S(1)}, f32[512]{0:T(512)}, u32[]{:S(2)}) copy-start(f32[512]{0:T(512)} %param.32) | copy-start | bytes 6148
  119.3 91.4 %all-reduce.12.cloned.1.call-start = ((), (), s32[]{:S(2)}) async-start(), calls=%async_computation.7 | async-start | bytes 1048576 | tf_op jit(solution)/shard_map/psum | solution.py:120
  122.0 142.5 %reduce-scatter.9.cloned.1.call-start = ((), (), s32[]{:S(2)}) async-start(), calls=%async_computation.10 | async-start | bytes 1310720 | tf_op jit(solution)/shard_map/reduce_scatter | solution.py:158
  210.7 3.2 copy-start.6
  210.7 4.5 copy-start.14
  214.1 1.1 copy-start.3
  223.7 58.7 %reduce-scatter.7.cloned.1.call-start = ((), (), s32[]{:S(2)}) async-start(), calls=%async_computation.9 | async-start | bytes 1310720 | tf_op jit(solution)/shard_map/reduce_scatter | solution.py:157
  240.4 5.4 %copy-start.26 = (f32[512]{0:T(512)S(1)}, f32[512]{0:T(512)}, u32[]{:S(2)}) copy-start(f32[512]{0:T(512)} %param.28) | copy-start | bytes 6148
  240.4 52.3 %reduce-scatter.13.cloned.1.call-start = ((), (), s32[]{:S(2)}) async-start(), calls=%async_computation.14 | async-start | bytes 393216 | tf_op jit(solution)/shard_map/reduce_scatter | solution.py:207
  242.7 62.0 %reduce-scatter.17.cloned.1.call-start = ((), (), s32[]{:S(2)}) async-start(), calls=%async_computation.16 | async-start | bytes 1572864 | tf_op jit(solution)/shard_map/reduce_scatter | solution.py:209
  245.7 71.0 %reduce-scatter.15.cloned.1.call-start = ((), (), s32[]{:S(2)}) async-start(), calls=%async_computation.15 | async-start | bytes 1572864 | tf_op jit(solution)/shard_map/reduce_scatter | solution.py:208
  248.9 80.2 %reduce-scatter.11.cloned.1.call-start = ((), (), s32[]{:S(2)}) async-start(), calls=%async_computation.13 | async-start | bytes 1179648 | tf_op jit(solution)/shard_map/reduce_scatter | solution.py:206
  288.2 96.7 %all-reduce.16.cloned.1.call-start = ((), (), s32[]{:S(2)}) async-start(), calls=%async_computation.11 | async-start | bytes 2097152 | tf_op jit(solution)/shard_map/psum | solution.py:172
  290.7 159.2 %all-reduce.20.cloned.1.call-start = ((), (), s32[]{:S(2)}) async-start(), calls=%async_computation.17 | async-start | bytes 3145728 | tf_op jit(solution)/shard_map/psum | solution.py:204
  329.1 186.1 %all-reduce.18.cloned.1.call-start = ((), (), s32[]{:S(2)}) async-start(), calls=%async_computation.12 | async-start | bytes 4096000 | tf_op jit(solution)/shard_map/psum | solution.py:202
  384.9 3.6 copy-start.4
  386.6 2.1 copy-start.27
  388.4 2.8 copy-start.28
  388.6 129.7 %copy-start.7 = (f32[512,512]{1,0:T(8,128)}, f32[512,512]{1,0:T(8,128)S(1)}, u32[]{:S(2)}) copy-start(f32[512,512]{1,0:T(8,128)S(1)} %add_add_fusion.2) | copy-start | bytes 3145732
  449.9 68.4 %copy-start.18 = (f32[256,128]{1,0:T(8,128)S(1)}, f32[256,128]{1,0:T(8,128)}, u32[]{:S(2)}) copy-start(f32[256,128]{1,0:T(8,128)} %get-tuple-element.125) | copy-start | bytes 393220
  515.2 3.8 copy-start.17
Sparse Core Ops, SparseCore 0:
  60.3 52.0 all-reduce.9
  119.4 51.1 all-reduce.13
  173.0 37.6 all-reduce.11
  223.8 27.7 reduce-scatter.8
  254.6 27.7 reduce-scatter.6
  285.0 7.6 reduce-scatter.12
  295.0 9.6 reduce-scatter.16
  307.0 9.6 reduce-scatter.14
  319.7 9.3 reduce-scatter.10
  331.9 52.9 all-reduce.15
  388.6 61.2 all-reduce.19
  453.6 61.5 all-reduce.17
